TPU v7x, 256 devices: a whole 4x4x8 slice. The times are simulated.
256 devices in a mesh: box: 64 (over x, z, core), col: 4 (over y).
Axes of the slice: x: 4, y: 4, z: 8, core: 2. Of those that a mesh axis runs over, the one named last changes fastest.
Arguments:
- leaf_maps: float32 [64, 1024, 1024], P('box', None, 'col'), as said below
- leaf_nodes: int32 [64, 4, 256], P('box'), may hold values from 0 to 255, each once within a row
Outputs:
- top_maps: float32 [64, 1024, 1024], P('box', None, 'col')
Inputs may be any that keep to these rules, and one draw needn't show every extreme that they name: `leaf_maps`: each leaf map is symmetric and positive definite. `leaf_nodes`: for each leaf and side, the entries are a permutation of 0 to 255.
All inputs are finite; a program needn't handle non-finite values.
Results may differ from a plain program's by a relative error of at most 0.0003.
Values sent between devices are 32-bit elements; how exact they have to be, the bound alone decides.
No kernel may reach another device: no remote copies, remote signals or barrier semaphores. Data moves between devices by JAX's collectives and lax.ppermute only.
A program may use at most 64 MiB of HBM per device.

v0:
```python
import jax
import jax.numpy as jnp
import numpy as np
from jax import lax
from jax.sharding import PartitionSpec as P

HALF_TABLE = ((0, 1, 1, 0), (0, 0, 1, 1), (1, 1, 0, 0), (1, 0, 0, 1))


def broadcast(block, axis, source):
    block = jnp.where(lax.axis_index(axis) == source, block, jnp.zeros_like(block))
    return lax.psum(block, axis)


def partner(value, axis, stride):
    return lax.ppermute(value, axis, [(i, i ^ 1 << stride) for i in range(lax.axis_size(axis))])


def cholesky_apply(factor, right_side):
    forward = lax.linalg.triangular_solve(factor, right_side, left_side=True, lower=True)
    return lax.linalg.triangular_solve(
        factor, forward, left_side=True, lower=True, transpose_a=True
    )


def highest_dot(left_matrix, right_matrix):
    return jnp.dot(
        left_matrix,
        right_matrix,
        precision=lax.Precision.HIGHEST,
        preferred_element_type=jnp.float32,
    )


def blocks(matrix, side_len, first_block, block_count):
    return matrix[first_block * side_len : (first_block + block_count) * side_len]


def shards(leaf_maps, leaf_nodes):
    side_len = leaf_maps.shape[2]
    leaf_panel = leaf_maps[0]
    side_nodes = leaf_nodes[0]
    box_place = lax.axis_index("box")
    column = lax.axis_index("col")
    sibling = box_place % 2
    pair_half = box_place // 2 % 2
    quarter = box_place % 4
    bases = (jnp.arange(4, dtype=jnp.int32) * side_len)[:, None]
    row_order = (bases + side_nodes).reshape(-1)
    own_nodes = jnp.take(side_nodes, column, axis=0)
    own_panel = jnp.take(jnp.take(leaf_panel, row_order, axis=0), own_nodes, axis=1)
    is_west = sibling == 0
    west_mask = is_west.astype(jnp.float32)
    east_mask = 1.0 - west_mask
    iface_own = broadcast(own_panel, "col", 1 + 2 * sibling)
    iface_peer = partner(iface_own, "box", 0)
    east_cols = jnp.where(is_west, iface_own, iface_peer)
    west_cols = jnp.where(is_west, iface_peer, iface_own)
    coupling = blocks(east_cols, side_len, 1, 1) + blocks(west_cols, side_len, 3, 1)
    coupling_rows = jnp.concatenate(
        [
            blocks(east_cols, side_len, 0, 1),
            blocks(west_cols, side_len, 0, 1),
            blocks(west_cols, side_len, 1, 1),
            blocks(east_cols, side_len, 2, 1),
            blocks(west_cols, side_len, 2, 1),
            blocks(east_cols, side_len, 3, 1),
        ],
        axis=0,
    )
    right_side = jnp.where(
        is_west, blocks(own_panel, side_len, 1, 1), blocks(own_panel, side_len, 3, 1)
    )
    diagonal_part = jnp.concatenate(
        [
            west_mask * blocks(own_panel, side_len, 0, 1),
            east_mask * blocks(own_panel, side_len, 0, 1),
            east_mask * blocks(own_panel, side_len, 1, 1),
            west_mask * blocks(own_panel, side_len, 2, 1),
            east_mask * blocks(own_panel, side_len, 2, 1),
            west_mask * blocks(own_panel, side_len, 3, 1),
        ],
        axis=0,
    )
    first_factor = jnp.linalg.cholesky(coupling)
    merged = diagonal_part - highest_dot(coupling_rows, cholesky_apply(first_factor, right_side))
    is_south = pair_half == 0
    root_col = jnp.where(is_south, 2, 0)
    half_own = broadcast(merged, "col", root_col)
    half_peer = partner(half_own, "box", 0)
    lower_half = jnp.where(is_west, half_own, half_peer)
    upper_half = jnp.where(is_west, half_peer, half_own)
    pair_stack = jnp.stack([lower_half, upper_half])
    other_stack = partner(pair_stack, "box", 1)
    own_pair = jnp.concatenate([pair_stack[0], pair_stack[1]], axis=1)
    other_pair = jnp.concatenate([other_stack[0], other_stack[1]], axis=1)
    north_cols = jnp.where(is_south, own_pair, other_pair)
    south_cols = jnp.where(is_south, other_pair, own_pair)
    coupling_two = blocks(north_cols, side_len, 3, 2) + blocks(south_cols, side_len, 0, 2)
    rows_two = jnp.concatenate(
        [
            blocks(north_cols, side_len, 0, 2),
            blocks(north_cols, side_len, 2, 1),
            blocks(south_cols, side_len, 2, 1),
            blocks(south_cols, side_len, 3, 2),
            blocks(north_cols, side_len, 5, 1),
            blocks(south_cols, side_len, 5, 1),
        ],
        axis=0,
    )
    second_factor = jnp.linalg.cholesky(coupling_two)
    holder = jnp.asarray(np.array(HALF_TABLE, dtype=np.int32))[quarter, column] == 0
    even_col = column % 2 == 0
    right_two = jnp.where(is_south, blocks(merged, side_len, 3, 2), blocks(merged, side_len, 0, 2))
    south_mask = is_south.astype(jnp.float32)
    north_mask = 1.0 - south_mask
    diag_two = jnp.concatenate(
        [
            south_mask * blocks(merged, side_len, 0, 2),
            south_mask * blocks(merged, side_len, 2, 1),
            north_mask * blocks(merged, side_len, 2, 1),
            north_mask * blocks(merged, side_len, 3, 2),
            south_mask * blocks(merged, side_len, 5, 1),
            north_mask * blocks(merged, side_len, 5, 1),
        ],
        axis=0,
    )
    solved, diag_two = (cholesky_apply(second_factor, right_two), diag_two)
    whole_panel = diag_two - highest_dot(rows_two, solved)
    top_rows = whole_panel[: 4 * side_len]
    bottom_rows = whole_panel[4 * side_len :]
    far_rows = partner(bottom_rows, "box", 1)
    near_rows = partner(bottom_rows, "box", 0)
    result = jnp.where(holder, top_rows, jnp.where(even_col, far_rows, near_rows))
    return result[None]


def solution(mesh):
    in_specs = (P("box", None, "col"), P("box", None, None))
    out_specs = P("box", None, "col")
    return jax.shard_map(shards, mesh=mesh, in_specs=in_specs, out_specs=out_specs, check_vma=False)
```

profile of v0, /device:TPU:2, one launch (start us, length us, event | category | flops | bytes accessed | tf_op | source)
XLA Modules:
  0.0 477.3 jit_solution(5407931225915577471)
XLA Ops:
  6.6 0.8 compare_select_fusion.2
  8.8 3.5 gather_fusion
  12.9 1.1 gather_fusion.1
  13.9 1.2 broadcast_select_fusion.3
  15.3 0.8 multiply_dynamic-update-slice_fusion.11
  16.0 0.8 multiply_dynamic-update-slice_fusion.10
  16.8 52.7 %all-reduce.5.cloned.1.call-done = f32[1024,256]{0,1:T(8,128)} async-done(((f32[1024,256]{0,1:T(8,128)}), f32[1024,256]{0,1:T(8,128)}) %all-reduce.5.cloned.1.call-update) | async-done | bytes 1048592 | tf_op jit(solution)/shard_map/psum | solution.py:12
  70.4 0.8 multiply_dynamic-update-slice_fusion.8
  71.2 0.8 slice_select_fusion.2
  72.0 0.8 multiply_dynamic-update-slice_fusion.6
  74.3 11.7 %cholesky.135 = f32[128,128]{1,0:T(8,128)S(1)} custom-call(f32[128,128]{1,0:T(8,128)S(1)} %copy.17), custom_call_target="Cholesky" | custom-call | tf_op jit(solution)/shard_map/jit(cholesky)/cholesky | solution.py:85
  86.1 9.8 %custom-call.46 = f32[1,128,128]{1,2,0:T(8,128)S(1)} custom-call(f32[1,128,128]{2,1,0:T(8,128)S(1)} %get-tuple-element.84), custom_call_target="InvertDiagBlocksLowerTriangular" | custom-call | tf_op jit(solution)/shard_map/jit(cholesky)/cholesky/custom-call.1 | solution.py:85
  95.9 1.1 constant_dynamic-update-slice_fusion.3
  97.0 1.1 convolution_subtract_fusion.11
  98.2 11.7 %cholesky.145 = f32[128,128]{1,0:T(8,128)S(1)} custom-call(f32[128,128]{1,0:T(8,128)S(1)} %copy.20), custom_call_target="Cholesky" | custom-call | tf_op jit(solution)/shard_map/jit(cholesky)/cholesky | solution.py:85
  112.6 4.0 while.3
  113.4 1.3 bitcast_dynamic-update-slice_fusion.4
  115.3 1.3 bitcast_dynamic-update-slice_fusion.4
  116.6 19.7 %custom-call.41 = f32[2,128,128]{1,2,0:T(8,128)S(1)} custom-call(f32[2,128,128]{2,1,0:T(8,128)S(1)} %get-tuple-element.21), custom_call_target="InvertDiagBlocksLowerTriangular" | custom-call | tf_op jit(solution)/shard_map/triangular_solve | solution.py:21
  138.2 4.8 broadcast_select_fusion
  143.0 56.9 %all-reduce.7.cloned.1.call-done = f32[1536,256]{0,1:T(8,128)} async-done(((f32[1536,256]{0,1:T(8,128)}), f32[1536,256]{0,1:T(8,128)}) %all-reduce.7.cloned.1.call-update) | async-done | bytes 1572880 | tf_op jit(solution)/shard_map/psum | solution.py:12
  199.8 3.6 collective-permute-done.1
  203.4 1.6 broadcast_select_fusion.2
  205.1 2.0 pad_maximum_fusion.1
  207.2 1.9 collective-permute-start.2
  209.1 1.2 multiply_dynamic-update-slice_fusion.1
  210.3 1.0 multiply_dynamic-update-slice_fusion.5
  211.4 1.0 slice_select_fusion.1
  212.4 1.3 copy-done.18
  213.7 64.3 %collective-permute-done.2 = f32[2,1536,256]{1,2,0:T(8,128)} collective-permute-done((f32[2,1536,256]{1,2,0:T(8,128)}, f32[2,1536,256]{1,2,0:T(8,128)}, u32[]{:S(2)}, u32[]{:S(2)}) %collective-permute-start.2) | collective-permute-done | bytes 3145760 | tf_op jit(solution)/shard_map/ppermute | solution.py:16
  278.0 2.1 slice_bitcast_fusion.1
  280.1 0.9 fusion.12
  281.0 1.7 copy-done.3
  282.7 0.9 copy-done.5
  284.3 1.0 copy-done.7
  285.3 11.7 %cholesky.276 = f32[128,128]{1,0:T(8,128)S(1)} custom-call(f32[128,128]{1,0:T(8,128)S(1)} %cholesky.342), custom_call_target="Cholesky" | custom-call | tf_op jit(solution)/shard_map/jit(cholesky)/cholesky | solution.py:111
  297.1 2.8 slice.325
  300.0 1.2 slice.326
  301.2 2.0 slice.327
  303.2 0.9 slice.328
  304.1 9.8 %custom-call.42 = f32[1,128,128]{1,2,0:T(8,128)S(1)} custom-call(f32[1,128,128]{2,1,0:T(8,128)S(1)} %get-tuple-element.80), custom_call_target="InvertDiagBlocksLowerTriangular" | custom-call | tf_op jit(solution)/shard_map/jit(cholesky)/cholesky | solution.py:111
  314.6 11.9 %cholesky.294 = f32[128,128]{1,0:T(8,128)S(1)} custom-call(f32[128,128]{1,0:T(8,128)S(1)} %cholesky.346), custom_call_target="Cholesky" | custom-call | tf_op jit(solution)/shard_map/jit(cholesky)/cholesky | solution.py:111
  327.8 9.8 %custom-call.43 = f32[1,128,128]{1,2,0:T(8,128)S(1)} custom-call(f32[1,128,128]{2,1,0:T(8,128)S(1)} %get-tuple-element.77), custom_call_target="InvertDiagBlocksLowerTriangular" | custom-call | tf_op jit(solution)/shard_map/jit(cholesky)/cholesky | solution.py:111
  338.2 11.7 %cholesky.315 = f32[128,128]{1,0:T(8,128)S(1)} custom-call(f32[128,128]{1,0:T(8,128)S(1)} %cholesky.351), custom_call_target="Cholesky" | custom-call | tf_op jit(solution)/shard_map/jit(cholesky)/cholesky | solution.py:111
  350.6 9.8 %custom-call.47 = f32[1,128,128]{1,2,0:T(8,128)S(1)} custom-call(f32[1,128,128]{2,1,0:T(8,128)S(1)} %get-tuple-element.74), custom_call_target="InvertDiagBlocksLowerTriangular" | custom-call | tf_op jit(solution)/shard_map/jit(cholesky)/cholesky/custom-call.1 | solution.py:111
  361.0 11.7 %cholesky.328 = f32[128,128]{1,0:T(8,128)S(1)} custom-call(f32[128,128]{1,0:T(8,128)S(1)} %convolution_subtract_fusion.12), custom_call_target="Cholesky" | custom-call | tf_op jit(solution)/shard_map/jit(cholesky)/cholesky | solution.py:111
  376.1 10.4 %while.4 = (s32[]{:T(128)}, f32[512,512]{1,0:T(8,128)S(1)}, s32[4,2]{0,1:T(2,128)S(1)}, f32[4,128,128]{2,1,0:T(8,128)}, s32[]{:T(128)}) while((s32[]{:T(128)}, f32[512,512]{1,0:T(8,128)S(1)}, s32[4,2]{0,1:T(2,128)S(1)}, f32[4,128,128]{2,1,0:T(8,128)}, s32[]{:T(128)}) %tuple.64), condition=%wide.while_cond.2, body=%wide.while_body.2.sunk | while | flops 2 | bytes 132705 | solution.py:21
  376.9 1.9 bitcast_dynamic-update-slice_fusion.5
  379.4 1.9 bitcast_dynamic-update-slice_fusion.5
  382.0 1.9 bitcast_dynamic-update-slice_fusion.5
  384.5 1.9 bitcast_dynamic-update-slice_fusion.5
  386.5 40.1 %custom-call.44 = f32[4,128,128]{1,2,0:T(8,128)S(1)} custom-call(f32[4,128,128]{2,1,0:T(8,128)} %get-tuple-element.29), custom_call_target="InvertDiagBlocksLowerTriangular" | custom-call | tf_op jit(solution)/shard_map/triangular_solve | solution.py:21
  426.6 1.2 fusion.51
  427.8 1.3 convolution_subtract_fusion.8
  430.4 0.8 convolution_subtract_fusion.4
  433.9 5.6 %fusion.8 = f32[2048,256]{0,1:T(8,128)S(1)} fusion(f32[2048,256]{0,1:T(8,128)} %copy-done.18, f32[256,512]{0,1:T(8,128)S(1)} %copy-done.17, f32[256,512]{0,1:T(8,128)S(1)} %copy-done.16, f32[768,512]{0,1:T(8,128)S(1)} %copy-done.12, f32[768,512]{0,1:T(8,128)S(1)} %copy-done.11, f32[128,256]{1,0:T(8,128)S(1)} %fusion.78, f32[128,256]{1,0:T(8,128)S(1)} %fusion.76, ...), kind=kOutput, calls=%fused_computation.18 | convolution fusion | flops 3225288704 | bytes 8912896 | tf_op jit(solution)/shard_map/dot_general | solution.py:27
  439.5 1.3 copy-done.9
  440.8 1.0 slice.332
  441.9 1.6 collective-permute-start.3
  443.4 1.3 dynamic_slice.3
  445.4 21.1 %collective-permute-done.3 = f32[1024,256]{0,1:T(8,128)S(1)} collective-permute-done((f32[1024,256]{0,1:T(8,128)}, f32[1024,256]{0,1:T(8,128)S(1)}, u32[]{:S(2)}, u32[]{:S(2)}) %collective-permute-start.3) | collective-permute-done | bytes 1048608 | tf_op jit(solution)/shard_map/ppermute | solution.py:16
  466.4 1.0 copy-done.14
  467.4 1.5 fusion.14
  468.9 1.3 copy.25
  (131 shorter events, 21.0 us)
Async XLA Ops:
  6.5 2.3 copy-start
  6.5 63.0 %all-reduce.5.cloned.1.call-start = ((), (), s32[]{:S(2)}) async-start(), calls=%async_computation | async-start | bytes 2097152 | tf_op jit(solution)/shard_map/psum | solution.py:12
  15.1 184.7 %all-reduce.7.cloned.1.call-start = ((), (), s32[]{:S(2)}) async-start(), calls=%async_computation.1 | async-start | bytes 3145728 | tf_op jit(solution)/shard_map/psum | solution.py:12
  69.5 3.3 copy-start.13
  69.5 3.3 collective-permute-start
  73.5 0.7 copy-start.15
  199.8 3.6 collective-permute-start.1
  205.1 2.1 copy-start.1
  207.2 70.8 %collective-permute-start.2 = (f32[2,1536,256]{1,2,0:T(8,128)}, f32[2,1536,256]{1,2,0:T(8,128)}, u32[]{:S(2)}, u32[]{:S(2)}) collective-permute-start(f32[2,1536,256]{1,2,0:T(8,128)} %pad_maximum_fusion.1), channel_id=1, source_target_pairs={{0,8},{4,12},{8,0},{12,4},{16,24},{20,28},{24,16},{28,20},{32,40},... | collective-permute-start | bytes 9437192 | tf_op jit(solution)/shard_map/ppermute | solution.py:16
  209.1 2.2 copy-start.6
  212.4 1.3 copy-start.18
  213.7 66.4 %copy-start.2 = (f32[1536,256]{0,1:T(8,128)S(1)}, f32[1536,256]{0,1:T(8,128)}, u32[]{:S(2)}) copy-start(f32[1536,256]{0,1:T(8,128)} %copy-done.1) | copy-start | bytes 4718596
  281.0 1.7 copy-start.3
  281.0 2.6 copy-start.5
  284.3 1.0 copy-start.7
  297.1 2.9 copy-start.4
  301.2 12.7 %copy-start.8 = (f32[512,512]{1,0:T(8,128)S(1)}, f32[512,512]{1,0:T(8,128)}, u32[]{:S(2)}) copy-start(f32[512,512]{1,0:T(8,128)} %copy-done.7) | copy-start | bytes 3145732
  376.1 53.4 %copy-start.10 = (f32[512,256]{0,1:T(8,128)S(1)}, f32[512,256]{0,1:T(8,128)}, u32[]{:S(2)}) copy-start(f32[512,256]{0,1:T(8,128)} %get-tuple-element.65) | copy-start | bytes 1572868
  430.4 3.5 copy-start.16
  430.4 3.5 copy-start.17
  431.5 2.4 copy-start.11
  431.5 2.4 copy-start.12
  439.5 1.3 copy-start.9
  441.9 24.6 %collective-permute-start.3 = (f32[1024,256]{0,1:T(8,128)}, f32[1024,256]{0,1:T(8,128)S(1)}, u32[]{:S(2)}, u32[]{:S(2)}) collective-permute-start(f32[1024,256]{0,1:T(8,128)} %slice.332), channel_id=1, source_target_pairs={{0,8},{4,12},{8,0},{12,4},{16,24},{20,28},{24,16},{28,20},{32,40},... | collective-permute-start | bytes 3145736 | tf_op jit(solution)/shard_map/ppermute | solution.py:16
  443.4 23.0 %collective-permute-start.4 = (f32[1024,256]{0,1:T(8,128)}, f32[1024,256]{0,1:T(8,128)S(1)}, u32[]{:S(2)}, u32[]{:S(2)}) collective-permute-start(f32[1024,256]{0,1:T(8,128)} %slice.332), channel_id=1, source_target_pairs={{0,4},{4,0},{8,12},{12,8},{16,20},{20,16},{24,28},{28,24},{32,36},... | collective-permute-start | bytes 3145736 | tf_op jit(solution)/shard_map/ppermute | solution.py:16
  466.4 1.0 copy-start.14
Sparse Core Ops, SparseCore 0:
  15.3 54.2 all-reduce.4
  143.1 56.6 all-reduce.6
where the time goes:
time: 480 us; the launch traced here: 477 us
  waiting for transfers between devices  199 us (41%)
  other arithmetic  190 us (40%)
  local copies, waits for them, and re-layouts  41.9 us (9%)
  matrix products  23.4 us (5%)
  between operations  18.7 us (4%)
    psum x2, waiting for transfers between devices, broadcast(): return lax.psum(block, axis)  110 us
    ppermute x5, waiting for transfers between devices, partner(): lax.ppermute(value, axis, [(i, i ^ 1 << stride) for i in range(lax.axis_s...  89 us
    another operation x15, other arithmetic, shards(): second_factor = jnp.linalg.cholesky(coupling_two)  79.2 us
    another operation x6, other arithmetic, cholesky_apply(): lax.linalg.triangular_solve(factor, forward, left_side=True, lower=True,...  60 us
    another operation x7, other arithmetic, shards(): first_factor = jnp.linalg.cholesky(coupling)  34.6 us
    another operation x18, local copies, waits for them, and re-layouts  13.9 us
    dot_general x2, matrix products, highest_dot(): jnp.dot(left_matrix, right_matrix, precision=lax.Precision.HIGHEST, prefe...  10.3 us
    unnamed x47, local copies, waits for them, and re-layouts  9.61 us
  transfers between devices with their start and end apart: 7, of which 5 were waited for; matrix products, arithmetic and copies ran while one was open for 2% of the time, Pallas kernels for 0%

commit v1 on v0

--- a/solution.py
+++ b/solution.py
@@ -7,9 +7,15 @@
 HALF_TABLE = ((0, 1, 1, 0), (0, 0, 1, 1), (1, 1, 0, 0), (1, 0, 0, 1))
 
 
+def add_all(x, name):
+    parts = lax.all_gather(x, name, axis=0, tiled=False)
+    total = parts.sum(axis=0)
+    return total
+
+
 def broadcast(block, axis, source):
     block = jnp.where(lax.axis_index(axis) == source, block, jnp.zeros_like(block))
-    return lax.psum(block, axis)
+    return add_all(block, axis)
 
 
 def partner(value, axis, stride):

time: 480 us -> 504 us (1.050)
  other arithmetic: 190 us -> 202 us
  waiting for transfers between devices: 199 us -> 209 us
    all_gather x0 -> x2, waiting for transfers between devices: none -> 121 us  [add_all(): parts = lax.all_gather(x, name, axis=0, tiled=False)]
    psum x2 -> x0, waiting for transfers between devices: 110 us -> none  [broadcast(): return lax.psum(block, axis)]
    reduce_sum x0 -> x2, other arithmetic: none -> 5.99 us  [add_all(): total = parts.sum(axis=0)]
    another operation x6, matrix products: 1.87 us -> 7.76 us  [shards(): second_factor = jnp.linalg.cholesky(coupling_two)]
where the time goes in v1:
time: 504 us; the launch traced here: 500 us
  waiting for transfers between devices  209 us (41%)
  other arithmetic  202 us (40%)
  local copies, waits for them, and re-layouts  38.5 us (8%)
  matrix products  27.2 us (5%)
  between operations  18.9 us (4%)
    all_gather x2, waiting for transfers between devices, add_all(): parts = lax.all_gather(x, name, axis=0, tiled=False)  121 us
    ppermute x5, waiting for transfers between devices, partner(): lax.ppermute(value, axis, [(i, i ^ 1 << stride) for i in range(lax.axis_s...  87.7 us
    another operation x15, other arithmetic, shards(): second_factor = jnp.linalg.cholesky(coupling_two)  81.2 us
    another operation x6, other arithmetic, cholesky_apply(): lax.linalg.triangular_solve(factor, forward, left_side=True, lower=True,...  60.4 us
    another operation x7, other arithmetic, shards(): first_factor = jnp.linalg.cholesky(coupling)  34.6 us
    dot_general x2, matrix products, highest_dot(): jnp.dot(left_matrix, right_matrix, precision=lax.Precision.HIGHEST, prefe...  12.9 us
    another operation x18, local copies, waits for them, and re-layouts  12 us
  transfers between devices with their start and end apart: 7, of which 5 were waited for; matrix products, arithmetic and copies ran while one was open for 2% of the time, Pallas kernels for 0%

profile of v1, /device:TPU:2, one launch (start us, length us, event | category | flops | bytes accessed | tf_op | source)
XLA Modules:
  0.0 499.8 jit_solution(8555787549502818260)
XLA Ops:
  8.8 3.5 gather_fusion
  12.8 1.1 gather_fusion.1
  14.3 1.1 fusion.15
  17.1 52.2 %all-gather.4.cloned.1.call-done = f32[4,1024,256]{2,1,0:T(8,128)} async-done(((f32[1,1024,256]{2,1,0:T(8,128)}), f32[4,1024,256]{2,1,0:T(8,128)}) %all-gather.4.cloned.1.call-update) | async-done | bytes 4194320 | tf_op jit(solution)/shard_map/all_gather | solution.py:11
  69.3 2.6 reduce_sum.18
  76.1 11.7 %cholesky.135 = f32[128,128]{1,0:T(8,128)S(1)} custom-call(f32[128,128]{1,0:T(8,128)S(1)} %cholesky.339), custom_call_target="Cholesky" | custom-call | tf_op jit(solution)/shard_map/jit(cholesky)/cholesky | solution.py:91
  87.8 9.8 %custom-call.46 = f32[1,128,128]{1,2,0:T(8,128)S(1)} custom-call(f32[1,128,128]{2,1,0:T(8,128)S(1)} %get-tuple-element.82), custom_call_target="InvertDiagBlocksLowerTriangular" | custom-call | tf_op jit(solution)/shard_map/jit(cholesky)/cholesky/custom-call.1 | solution.py:91
  98.1 11.7 %cholesky.145 = f32[128,128]{1,0:T(8,128)S(1)} custom-call(f32[128,128]{1,0:T(8,128)S(1)} %convolution_subtract_fusion.11), custom_call_target="Cholesky" | custom-call | tf_op jit(solution)/shard_map/jit(cholesky)/cholesky | solution.py:91
  112.7 4.3 while.3
  113.5 1.4 bitcast_dynamic-update-slice_fusion.4
  115.5 1.4 bitcast_dynamic-update-slice_fusion.4
  116.9 19.7 %custom-call.41 = f32[2,128,128]{1,2,0:T(8,128)S(1)} custom-call(f32[2,128,128]{2,1,0:T(8,128)S(1)} %get-tuple-element.21), custom_call_target="InvertDiagBlocksLowerTriangular" | custom-call | tf_op jit(solution)/shard_map/triangular_solve | solution.py:27
  138.4 5.8 %broadcast_select_fusion = (f32[1536,256]{1,0:T(8,128)}, f32[1536,256]{1,0:T(8,128)}) fusion(pred[]{:T(512)S(6)} %eq.31, f32[1536,256]{1,0:T(8,128)} %multiply_dynamic-update-slice_fusion.6, f32[1536,256]{0,1:T(8,128)S(1)} %get-tuple-element.66, f32[128,256]{1,0:T(8,128)S(1)} %fusion.72, f32[128,256]{1,0:T(8,128)S(1)} %fusion.71), kind=kOutput, calls=%fused_computation.49 | convolution fusion | flops 1208811520 | bytes 6553601 | tf_op jit(solution)/shard_map/dot_general | solution.py:33
  144.2 68.8 %all-gather.6.cloned.1.call-done = f32[6144,256]{1,0:T(8,128)} async-done(((f32[1536,256]{1,0:T(8,128)}), f32[6144,256]{1,0:T(8,128)}) %all-gather.6.cloned.1.call-update) | async-done | bytes 6291472 | tf_op jit(solution)/shard_map/all_gather | solution.py:11
  213.0 3.4 reduce_sum.19
  217.0 1.0 copy-done.7
  218.0 2.4 collective-permute-done.1
  220.4 1.7 broadcast_select_fusion.2
  222.1 1.8 pad_maximum_fusion.1
  223.9 1.9 collective-permute-start.2
  225.9 1.2 multiply_dynamic-update-slice_fusion.1
  227.1 1.0 multiply_dynamic-update-slice_fusion.5
  228.1 0.9 slice_select_fusion.1
  229.0 1.3 copy-done.14
  230.4 64.4 %collective-permute-done.2 = f32[2,1536,256]{1,2,0:T(8,128)} collective-permute-done((f32[2,1536,256]{1,2,0:T(8,128)}, f32[2,1536,256]{1,2,0:T(8,128)}, u32[]{:S(2)}, u32[]{:S(2)}) %collective-permute-start.2) | collective-permute-done | bytes 3145760 | tf_op jit(solution)/shard_map/ppermute | solution.py:22
  294.8 2.1 slice_bitcast_fusion.1
  296.8 0.9 fusion.12
  297.7 1.6 copy-done.2
  299.4 1.0 copy-done.4
  300.4 1.1 slice_add_fusion
  301.5 2.6 copy.26
  304.1 1.9 fusion.16
  306.0 1.1 copy-done.8
  307.1 11.7 %cholesky.276 = f32[128,128]{1,0:T(8,128)S(1)} custom-call(f32[128,128]{1,0:T(8,128)S(1)} %cholesky.342), custom_call_target="Cholesky" | custom-call | tf_op jit(solution)/shard_map/jit(cholesky)/cholesky | solution.py:117
  318.8 1.1 cholesky.301
  320.0 1.3 slice.325
  321.2 1.2 copy-done.3
  322.4 1.3 slice.326
  323.7 0.8 slice.327
  324.5 0.8 slice.328
  325.3 9.8 %custom-call.42 = f32[1,128,128]{1,2,0:T(8,128)S(1)} custom-call(f32[1,128,128]{2,1,0:T(8,128)S(1)} %get-tuple-element.78), custom_call_target="InvertDiagBlocksLowerTriangular" | custom-call | tf_op jit(solution)/shard_map/jit(cholesky)/cholesky | solution.py:117
  335.2 1.9 constant_dynamic-update-slice_fusion.1
  337.1 1.2 convolution_subtract_fusion.1
  338.3 11.8 %cholesky.294 = f32[128,128]{1,0:T(8,128)S(1)} custom-call(f32[128,128]{1,0:T(8,128)S(1)} %cholesky.346), custom_call_target="Cholesky" | custom-call | tf_op jit(solution)/shard_map/jit(cholesky)/cholesky | solution.py:117
  352.1 9.8 %custom-call.43 = f32[1,128,128]{1,2,0:T(8,128)S(1)} custom-call(f32[1,128,128]{2,1,0:T(8,128)S(1)} %get-tuple-element.75), custom_call_target="InvertDiagBlocksLowerTriangular" | custom-call | tf_op jit(solution)/shard_map/jit(cholesky)/cholesky | solution.py:117
  362.0 0.9 convolution_dynamic-update-slice_fusion
  362.9 1.4 convolution_subtract_fusion.6
  364.3 11.7 %cholesky.315 = f32[128,128]{1,0:T(8,128)S(1)} custom-call(f32[128,128]{1,0:T(8,128)S(1)} %cholesky.351), custom_call_target="Cholesky" | custom-call | tf_op jit(solution)/shard_map/jit(cholesky)/cholesky | solution.py:117
  377.3 9.8 %custom-call.47 = f32[1,128,128]{1,2,0:T(8,128)S(1)} custom-call(f32[1,128,128]{2,1,0:T(8,128)S(1)} %get-tuple-element.72), custom_call_target="InvertDiagBlocksLowerTriangular" | custom-call | tf_op jit(solution)/shard_map/jit(cholesky)/cholesky/custom-call.1 | solution.py:117
  387.2 0.8 fusion.13
  388.0 1.4 convolution_subtract_fusion.12
  389.4 11.9 %cholesky.328 = f32[128,128]{1,0:T(8,128)S(1)} custom-call(f32[128,128]{1,0:T(8,128)S(1)} %convolution_subtract_fusion.12), custom_call_target="Cholesky" | custom-call | tf_op jit(solution)/shard_map/jit(cholesky)/cholesky | solution.py:117
  405.1 1.4 select_select_fusion
  406.5 8.1 %while.4 = (s32[]{:T(128)}, f32[512,512]{1,0:T(8,128)S(1)}, s32[4,2]{0,1:T(2,128)S(1)}, f32[4,128,128]{2,1,0:T(8,128)S(1)}, s32[]{:T(128)}) while((s32[]{:T(128)}, f32[512,512]{1,0:T(8,128)S(1)}, s32[4,2]{0,1:T(2,128)S(1)}, f32[4,128,128]{2,1,0:T(8,128)S(1)}, s32[]{:T(128)}) %tuple.63), condition=%wide.while_cond.2, body=%wide.while_body.2.sunk | while | flops 2 | bytes 131181 | solution.py:27
  407.1 1.4 bitcast_dynamic-update-slice_fusion.5
  409.2 1.4 bitcast_dynamic-update-slice_fusion.5
  411.2 1.4 bitcast_dynamic-update-slice_fusion.5
  413.2 1.4 bitcast_dynamic-update-slice_fusion.5
  414.6 39.3 %custom-call.44 = f32[4,128,128]{1,2,0:T(8,128)S(1)} custom-call(f32[4,128,128]{2,1,0:T(8,128)S(1)} %get-tuple-element.29), custom_call_target="InvertDiagBlocksLowerTriangular" | custom-call | tf_op jit(solution)/shard_map/triangular_solve | solution.py:27
  458.5 7.1 %fusion.8 = f32[2048,256]{1,0:T(8,128)S(1)} fusion(f32[2048,256]{1,0:T(8,128)S(1)} %copy-done.15, f32[256,512]{0,1:T(8,128)S(1)} %copy-done.13, f32[256,512]{0,1:T(8,128)S(1)} %copy-done.12, f32[768,512]{0,1:T(8,128)S(1)} %copy-done.11, f32[768,512]{0,1:T(8,128)S(1)} %copy-done.10, f32[128,256]{1,0:T(8,128)S(1)} %fusion.79, f32[128,256]{1,0:T(8,128)S(1)} %fusion.77, ...), kind=kOutput, calls=%fused_computation.18 | convolution fusion | flops 3225288704 | bytes 8912896 | tf_op jit(solution)/shard_map/dot_general | solution.py:33
  465.7 1.7 collective-permute-start.3
  467.4 1.3 dynamic_slice.3
  469.3 21.0 %collective-permute-done.3 = f32[1024,256]{1,0:T(8,128)} collective-permute-done((f32[1024,256]{1,0:T(8,128)S(1)}, f32[1024,256]{1,0:T(8,128)}, u32[]{:S(2)}, u32[]{:S(2)}) %collective-permute-start.3) | collective-permute-done | bytes 1048608 | tf_op jit(solution)/shard_map/ppermute | solution.py:22
  490.3 2.5 fusion.14
  (128 shorter events, 26.1 us)
Async XLA Ops:
  6.5 2.3 copy-start
  6.5 62.7 %all-gather.4.cloned.1.call-start = ((), (), s32[]{:S(2)}) async-start(), calls=%async_computation | async-start | bytes 5242880 | tf_op jit(solution)/shard_map/all_gather | solution.py:11
  15.4 197.6 %all-gather.6.cloned.1.call-start = ((), (), s32[]{:S(2)}) async-start(), calls=%async_computation.1 | async-start | bytes 7864320 | tf_op jit(solution)/shard_map/all_gather | solution.py:11
  72.2 3.2 collective-permute-start
  216.9 1.1 copy-start.7
  216.9 3.5 collective-permute-start.1
  223.9 70.8 %collective-permute-start.2 = (f32[2,1536,256]{1,2,0:T(8,128)}, f32[2,1536,256]{1,2,0:T(8,128)}, u32[]{:S(2)}, u32[]{:S(2)}) collective-permute-start(f32[2,1536,256]{1,2,0:T(8,128)} %pad_maximum_fusion.1), channel_id=1, source_target_pairs={{0,8},{4,12},{8,0},{12,4},{16,24},{20,28},{24,16},{28,20},{32,40},... | collective-permute-start | bytes 9437192 | tf_op jit(solution)/shard_map/ppermute | solution.py:22
  225.9 2.2 copy-start.6
  229.0 1.4 copy-start.14
  297.7 1.6 copy-start.2
  297.7 2.7 copy-start.4
  304.1 15.9 %copy-start.5 = (f32[1536,512]{0,1:T(8,128)S(1)}, f32[1536,512]{0,1:T(8,128)}, u32[]{:S(2)}) copy-start(f32[1536,512]{0,1:T(8,128)} %copy-done.4) | copy-start | bytes 9437188
  306.0 1.1 copy-start.8
  319.9 2.5 copy-start.3
  389.4 64.5 %copy-start.9 = (f32[512,256]{1,0:T(8,128)S(1)}, f32[512,256]{1,0:T(8,128)}, u32[]{:S(2)}) copy-start(f32[512,256]{1,0:T(8,128)} %get-tuple-element.63) | copy-start | bytes 1572868
  453.9 4.6 copy-start.15
  455.4 3.1 copy-start.12
  455.4 3.1 copy-start.13
  456.2 2.4 copy-start.10
  456.2 2.4 copy-start.11
  465.7 24.6 %collective-permute-start.3 = (f32[1024,256]{1,0:T(8,128)S(1)}, f32[1024,256]{1,0:T(8,128)}, u32[]{:S(2)}, u32[]{:S(2)}) collective-permute-start(f32[1024,256]{1,0:T(8,128)S(1)} %slice.332), channel_id=1, source_target_pairs={{0,8},{4,12},{8,0},{12,4},{16,24},{20,28},{24,16},{28,20},{32,40},... | collective-permute-start | bytes 3145736 | tf_op jit(solution)/shard_map/ppermute | solution.py:22
  467.4 22.9 %collective-permute-start.4 = (f32[1024,256]{1,0:T(8,128)S(1)}, f32[1024,256]{1,0:T(8,128)}, u32[]{:S(2)}, u32[]{:S(2)}) collective-permute-start(f32[1024,256]{1,0:T(8,128)S(1)} %slice.332), channel_id=1, source_target_pairs={{0,4},{4,0},{8,12},{12,8},{16,20},{20,16},{24,28},{28,24},{32,36},... | collective-permute-start | bytes 3145736 | tf_op jit(solution)/shard_map/ppermute | solution.py:22
  490.3 2.5 copy-start.1
Sparse Core Ops, SparseCore 0:
  15.5 53.7 all-gather.3
  144.3 68.6 all-gather.5
